TPU v7x, 32 devices: a whole 2x2x4 slice. The times are simulated.
32 devices in a mesh: outer: 4 (over y, core), inner: 8 (over z, x).
Axes of the slice: x: 2, y: 2, z: 4, core: 2. Of those that a mesh axis runs over, the one named last changes fastest.
Arguments:
- queries: bfloat16 [4096, 2048], P(('outer', 'inner')), may hold values from -6 to 6
- keys: bfloat16 [4096, 2048], P(('outer', 'inner')), may hold values from -6 to 6
- values: bfloat16 [4096, 2048], P(('outer', 'inner')), may hold values from -6 to 6
- gain: float32 [2048], replicated, may hold values from 0.5 to 1.5
Outputs:
- attended: bfloat16 [4096, 2048], P(('outer', 'inner'))
All inputs are finite; a program needn't handle non-finite values.
Results may differ from a plain program's by a relative error of at most 0.0049.
Values sent between devices are 32-bit elements; how exact they have to be, the bound alone decides.
No kernel may reach another device: no remote copies, remote signals or barrier semaphores. Data moves between devices by JAX's collectives and lax.ppermute only.
A program may use at most 64 MiB of HBM per device.

v0:
```python
import jax
import jax.numpy as jnp
from jax import lax
from jax.sharding import PartitionSpec as P

HEADS = 16
HEAD_DIM = 128
STRETCH = 128


def entering(value, axis, join, neutral):
    count, mine = (lax.axis_size(axis), lax.axis_index(axis))
    pieces = lax.all_gather(value, axis)
    running = jnp.full_like(value, 0) + jnp.asarray(neutral, value.dtype)

    def turn(position, running):
        longer = join(running, pieces[position])
        return jnp.where(position < mine, longer, running)

    return lax.fori_loop(0, count - 1, turn, running)


def add_states(earlier, later):
    return earlier + later


def on_device(queries, keys, values, gain):
    tok_rows = queries.shape[0]
    nblocks = tok_rows // STRETCH
    q_blocks = queries.reshape(nblocks, STRETCH, HEADS, HEAD_DIM)
    k_blocks = keys.reshape(nblocks, STRETCH, HEADS, HEAD_DIM)
    v_blocks = values.reshape(nblocks, STRETCH, HEADS, HEAD_DIM)
    block_states = jnp.einsum(
        "ckhd,ckhe->chde", k_blocks, v_blocks, preferred_element_type=jnp.float32
    )
    own_state = jnp.sum(block_states, axis=0)
    zero_state = jnp.zeros_like(own_state)
    within = entering(own_state, "inner", add_states, zero_state)
    share = lax.psum_scatter(own_state, "inner", scatter_dimension=1, tiled=True)
    share_before = entering(share, "outer", add_states, jnp.zeros_like(share))
    before = lax.all_gather(share_before, "inner", axis=1, tiled=True)
    incoming = before + within
    local_before = jnp.concatenate(
        [jnp.zeros_like(block_states), jnp.cumsum(block_states[:-1], axis=0)], axis=0
    )
    carried_bf = (incoming[None] + local_before).astype(jnp.bfloat16)
    causal = jnp.arange(STRETCH)[:, None] >= jnp.arange(STRETCH)[None, :]
    scores = jnp.einsum("cqhd,ckhd->chqk", q_blocks, k_blocks, preferred_element_type=jnp.float32)
    scores = jnp.where(causal[None, None], scores, 0.0).astype(jnp.bfloat16)
    raw = jnp.einsum("chqk,ckhd->cqhd", scores, v_blocks, preferred_element_type=jnp.float32)
    raw = raw + jnp.einsum(
        "cqhd,chde->cqhe", q_blocks, carried_bf, preferred_element_type=jnp.float32
    )
    scale = lax.rsqrt(jnp.mean(raw * raw, axis=-1, keepdims=True) + 1e-06)
    normed = raw * scale * gain.reshape(HEADS, HEAD_DIM)[None, None]
    return normed.astype(jnp.bfloat16).reshape(tok_rows, HEADS * HEAD_DIM)


def solution(mesh):
    return jax.shard_map(
        on_device,
        mesh=mesh,
        in_specs=(
            P(("outer", "inner"), None),
            P(("outer", "inner"), None),
            P(("outer", "inner"), None),
            P(),
        ),
        out_specs=P(("outer", "inner"), None),
        check_vma=False,
    )
```

profile of v0, /device:TPU:0, one launch (start us, length us, event | category | flops | bytes accessed | tf_op | source)
XLA Modules:
  0.0 253.1 jit_solution(3675425433769225967)
XLA Ops:
  6.5 0.0 copy-start
  6.5 0.0 reduce-scatter.2.cloned.1.call-start
  6.5 1.4 copy.18
  7.9 2.3 fusion.3
  10.2 0.0 reduce-scatter.2.cloned.1.call-update
  10.2 0.0 all-gather.7.cloned.1.call-start
  10.3 0.7 all-gather.7.cloned.1.call-update
  11.0 0.0 all-gather.5.cloned.1.call-start
  11.1 0.0 copy-done
  11.1 1.7 convolution_bitcast_fusion
  12.8 65.4 %reduce-scatter.2.cloned.1.call-done = f32[16,16,128]{2,1,0:T(8,128)} async-done(((f32[16,128,128]{2,1,0:T(8,128)}), f32[16,16,128]{2,1,0:T(8,128)}) %reduce-scatter.2.cloned.1.call-update) | async-done | bytes 131088 | tf_op jit(solution)/shard_map/reduce_scatter | solution.py:39
  78.2 7.3 %all-gather = f32[64,16,128]{2,1,0:T(8,128)S(1)} all-gather(f32[16,16,128]{2,1,0:T(8,128)} %reduce-scatter.2.cloned.1.call-done), channel_id=2, replica_groups=mesh['outer'=4,'inner'=8] {'outer'}, dimensions={0}, use_global_device_ids=true | all-gather | bytes 655360 | tf_op jit(solution)/shard_map/all_gather | solution.py:13
  85.5 0.2 while.28
  85.7 0.0 copy-start.1
  85.7 0.6 copy-done.1
  86.4 0.0 all-gather.5.cloned.1.call-update
  86.4 117.4 %all-gather.7.cloned.1.call-done = f32[128,128,128]{2,1,0:T(8,128)} async-done(((f32[16,128,128]{2,1,0:T(8,128)}), f32[128,128,128]{2,1,0:T(8,128)}) %all-gather.7.cloned.1.call-update) | async-done | bytes 8388624 | tf_op jit(solution)/shard_map/all_gather | solution.py:13
  203.8 0.0 copy-start.2
  203.8 11.3 %while.29 = (s32[]{:T(128)}, f32[16,128,128]{2,1,0:T(8,128)S(1)}, s32[]{:T(128)}, f32[8,16,128,128]{3,2,1,0:T(8,128)}, s32[]{:T(128)}, /*index=5*/s32[]{:T(128)}) while((s32[]{:T(128)}, f32[16,128,128]{2,1,0:T(8,128)S(1)}, s32[]{:T(128)}, f32[8,16,128,128]{3,2,1,0:T(8,128)}, s32[]{:T(128)}, /*index=5*/s32[]{:T(128)}) %tuple.72), condition=%wide.region_4.5_spmd.clone, body=%wide.region_3.4_spmd.clone.sunk | while | flops 786436 | bytes 3145821 | solution.py:20
  203.8 1.6 add_select_fusion.5
  205.4 1.6 add_select_fusion.5
  207.0 1.6 add_select_fusion.5
  208.6 1.6 add_select_fusion.5
  210.3 1.6 add_select_fusion.5
  211.9 1.6 add_select_fusion.5
  213.5 1.6 add_select_fusion.5
  215.1 28.3 %all-gather.5.cloned.1.call-done = f32[16,128,128]{2,1,0:T(8,128)} async-done(((f32[16,16,128]{2,1,0:T(8,128)}), f32[16,128,128]{2,1,0:T(8,128)}) %all-gather.5.cloned.1.call-update) | async-done | bytes 1048592 | tf_op jit(solution)/shard_map/all_gather | solution.py:41
  243.4 1.7 multiply_reduce_fusion
  245.2 0.0 copy-done.2
  245.2 0.3 multiply_convert_fusion
  245.6 1.0 copy.16
  (7 shorter events, 0.1 us)
Async XLA Ops:
  6.5 4.6 %copy-start = (bf16[128,2048]{1,0:T(8,128)(2,1)S(1)}, bf16[128,2048]{1,0:T(8,128)(2,1)}, u32[]{:S(2)}) copy-start(bf16[128,2048]{1,0:T(8,128)(2,1)} %param.8) | copy-start | bytes 1572868
  6.5 71.7 %reduce-scatter.2.cloned.1.call-start = ((), (), s32[]{:S(2)}) async-start(), calls=%async_computation.1 | async-start | bytes 1179648 | tf_op jit(solution)/shard_map/reduce_scatter | solution.py:39
  10.2 193.5 %all-gather.7.cloned.1.call-start = ((), (), s32[]{:S(2)}) async-start(), calls=%async_computation.3 | async-start | bytes 9437184 | tf_op jit(solution)/shard_map/all_gather | solution.py:13
  11.0 232.5 %all-gather.5.cloned.1.call-start = ((), (), s32[]{:S(2)}) async-start(), calls=%async_computation.2 | async-start | bytes 1179648 | tf_op jit(solution)/shard_map/all_gather | solution.py:41
  85.7 0.7 copy-start.1
  203.8 41.4 %copy-start.2 = (f32[2048]{0:T(1024)S(1)}, f32[2048]{0:T(1024)}, u32[]{:S(2)}) copy-start(f32[2048]{0:T(1024)} %param.11) | copy-start | bytes 24580
Sparse Core Ops, SparseCore 0:
  10.7 67.4 reduce-scatter.1
  80.3 123.3 all-gather.6
  205.8 37.5 all-gather.4
where the time goes:
time: 254 us; the launch traced here: 253 us
  waiting for transfers between devices  212 us (83%)
  between operations  13.2 us (5%)
  other arithmetic  11.7 us (5%)
  blocking collectives  7.33 us (3%)
  matrix products  5.74 us (2%)
  local copies, waits for them, and re-layouts  3.03 us (1%)
    all_gather x1, waiting for transfers between devices, entering(): pieces = lax.all_gather(value, axis)  117 us
    reduce_scatter x1, waiting for transfers between devices, on_device(): lax.psum_scatter(own_state, 'inner', scatter_dimension=1, tiled=True)  65.4 us
    all_gather x1, waiting for transfers between devices, on_device(): before = lax.all_gather(share_before, 'inner', axis=1, tiled=True)  28.3 us
    select_n x10, other arithmetic, turn(): return jnp.where(position < mine, longer, running)  11.3 us
    all_gather x1, blocking collectives, entering(): pieces = lax.all_gather(value, axis)  7.33 us
  transfers between devices with their start and end apart: 3, of which 3 were waited for; matrix products, arithmetic and copies ran while one was open for 5% of the time, Pallas kernels for 0%

commit v1 on v0

--- a/solution.py
+++ b/solution.py
@@ -38,7 +38,14 @@
     within = entering(own_state, "inner", add_states, zero_state)
     share = lax.psum_scatter(own_state, "inner", scatter_dimension=1, tiled=True)
     share_before = entering(share, "outer", add_states, jnp.zeros_like(share))
-    before = lax.all_gather(share_before, "inner", axis=1, tiled=True)
+    ring = [share_before]
+    for hop in range(7):
+        ring.append(lax.ppermute(ring[-1], "inner", [(dev, (dev + 1) % 8) for dev in range(8)]))
+    before = jnp.roll(
+        jnp.concatenate(ring[::-1], axis=1),
+        (lax.axis_index("inner") + 1) * ring[0].shape[1],
+        axis=1,
+    )
     incoming = before + within
     local_before = jnp.concatenate(
         [jnp.zeros_like(block_states), jnp.cumsum(block_states[:-1], axis=0)], axis=0

time: 254 us -> 240 us (0.945)
  waiting for transfers between devices: 212 us -> 181 us
  local copies, waits for them, and re-layouts: 3.03 us -> 19.7 us
    all_gather x1, waiting for transfers between devices: 117 us -> 43.9 us  [entering(): pieces = lax.all_gather(value, axis)]
    ppermute x0 -> x7, waiting for transfers between devices: none -> 69.5 us  [on_device(): lax.ppermute(ring[-1], 'inner', [(dev, (dev + 1) % 8) for dev in range(8)])]
    all_gather x1 -> x0, waiting for transfers between devices: 28.3 us -> none  [on_device(): before = lax.all_gather(share_before, 'inner', axis=1, tiled=True)]
    unnamed x6 -> x33, local copies, waits for them, and re-layouts: 0.66 us -> 16.6 us
  transfers between devices with their start and end apart: 3 -> 9, of which waited for: 3 -> 9; matrix products, arithmetic and copies ran while one was open for 5% -> 8% of each run, Pallas kernels for 0% -> 0%
where the time goes in v1:
time: 240 us
  waiting for transfers between devices  181 us (75%)
  local copies, waits for them, and re-layouts  19.7 us (8%)
  between operations  13.6 us (6%)
  other arithmetic  11.6 us (5%)
  blocking collectives  7.33 us (3%)
  matrix products  4.73 us (2%)
    ppermute x7, waiting for transfers between devices, on_device(): lax.ppermute(ring[-1], 'inner', [(dev, (dev + 1) % 8) for dev in range(8)])  69.5 us
    reduce_scatter x1, waiting for transfers between devices, on_device(): lax.psum_scatter(own_state, 'inner', scatter_dimension=1, tiled=True)  67.2 us
    all_gather x1, waiting for transfers between devices, entering(): pieces = lax.all_gather(value, axis)  43.9 us
    unnamed x33, local copies, waits for them, and re-layouts  16.6 us
    select_n x10, other arithmetic, turn(): return jnp.where(position < mine, longer, running)  11.2 us
    all_gather x1, blocking collectives, entering(): pieces = lax.all_gather(value, axis)  7.33 us
  transfers between devices with their start and end apart: 9, of which 9 were waited for; matrix products, arithmetic and copies ran while one was open for 8% of the time, Pallas kernels for 0%

profile of v1, /device:TPU:0, one launch (start us, length us, event | category | flops | bytes accessed | tf_op | source)
XLA Modules:
  0.0 239.6 jit_solution(1578989103899441874)
XLA Ops:
  6.5 1.4 copy.18
  7.9 2.3 fusion.3
  10.2 0.0 reduce-scatter.2.cloned.1.call-update
  10.2 0.0 copy-start.1
  10.3 0.0 all-gather.4.cloned.1.call-start
  10.3 0.7 all-gather.4.cloned.1.call-update
  11.0 67.2 %reduce-scatter.2.cloned.1.call-done = f32[16,16,128]{2,1,0:T(8,128)} async-done(((f32[16,128,128]{2,1,0:T(8,128)}), f32[16,16,128]{2,1,0:T(8,128)}) %reduce-scatter.2.cloned.1.call-update) | async-done | bytes 131088 | tf_op jit(solution)/shard_map/reduce_scatter | solution.py:39
  78.2 7.3 %all-gather = f32[64,16,128]{2,1,0:T(8,128)S(1)} all-gather(f32[16,16,128]{2,1,0:T(8,128)} %reduce-scatter.2.cloned.1.call-done), channel_id=2, replica_groups=mesh['outer'=4,'inner'=8] {'outer'}, dimensions={0}, use_global_device_ids=true | all-gather | bytes 655360 | tf_op jit(solution)/shard_map/all_gather | solution.py:13
  85.5 0.2 while.28
  85.7 1.2 collective-permute-start
  86.9 8.5 %collective-permute-done = f32[16,16,128]{2,1,0:T(8,128)S(1)} collective-permute-done((f32[16,16,128]{2,1,0:T(8,128)S(1)}, f32[16,16,128]{2,1,0:T(8,128)S(1)}, u32[]{:S(2)}, u32[]{:S(2)}) %collective-permute-start) | collective-permute-done | bytes 131104 | tf_op jit(solution)/shard_map/ppermute | solution.py:43
  95.4 11.0 %collective-permute-done.1 = f32[16,16,128]{2,1,0:T(8,128)S(1)} collective-permute-done((f32[16,16,128]{2,1,0:T(8,128)S(1)}, f32[16,16,128]{2,1,0:T(8,128)S(1)}, u32[]{:S(2)}, u32[]{:S(2)}) %collective-permute-start.1) | collective-permute-done | bytes 131104 | tf_op jit(solution)/shard_map/ppermute | solution.py:43
  106.4 10.8 %collective-permute-done.2 = f32[16,16,128]{2,1,0:T(8,128)S(1)} collective-permute-done((f32[16,16,128]{2,1,0:T(8,128)S(1)}, f32[16,16,128]{2,1,0:T(8,128)S(1)}, u32[]{:S(2)}, u32[]{:S(2)}) %collective-permute-start.2) | collective-permute-done | bytes 131104 | tf_op jit(solution)/shard_map/ppermute | solution.py:43
  117.2 10.6 %collective-permute-done.3 = f32[16,16,128]{2,1,0:T(8,128)S(1)} collective-permute-done((f32[16,16,128]{2,1,0:T(8,128)S(1)}, f32[16,16,128]{2,1,0:T(8,128)S(1)}, u32[]{:S(2)}, u32[]{:S(2)}) %collective-permute-start.3) | collective-permute-done | bytes 131104 | tf_op jit(solution)/shard_map/ppermute | solution.py:43
  127.8 10.6 %collective-permute-done.4 = f32[16,16,128]{2,1,0:T(8,128)S(1)} collective-permute-done((f32[16,16,128]{2,1,0:T(8,128)S(1)}, f32[16,16,128]{2,1,0:T(8,128)S(1)}, u32[]{:S(2)}, u32[]{:S(2)}) %collective-permute-start.4) | collective-permute-done | bytes 131104 | tf_op jit(solution)/shard_map/ppermute | solution.py:43
  138.4 7.8 %collective-permute-done.5 = f32[16,16,128]{2,1,0:T(8,128)} collective-permute-done((f32[16,16,128]{2,1,0:T(8,128)S(1)}, f32[16,16,128]{2,1,0:T(8,128)}, u32[]{:S(2)}, u32[]{:S(2)}) %collective-permute-start.5) | collective-permute-done | bytes 131104 | tf_op jit(solution)/shard_map/ppermute | solution.py:43
  146.2 0.7 convolution_bitcast_fusion
  146.9 0.0 copy-start.7
  147.0 10.2 %collective-permute-done.6 = f32[16,16,128]{2,1,0:T(8,128)} collective-permute-done((f32[16,16,128]{2,1,0:T(8,128)}, f32[16,16,128]{2,1,0:T(8,128)}, u32[]{:S(2)}, u32[]{:S(2)}) %collective-permute-start.6) | collective-permute-done | bytes 131104 | tf_op jit(solution)/shard_map/ppermute | solution.py:43
  157.1 1.6 constant_dynamic-update-slice_fusion.15
  158.7 1.6 constant_dynamic-update-slice_fusion.14
  160.3 1.6 constant_dynamic-update-slice_fusion.13
  161.9 1.6 constant_dynamic-update-slice_fusion.12
  163.4 1.6 constant_dynamic-update-slice_fusion.11
  165.0 0.7 constant_dynamic-update-slice_fusion.10
  165.7 0.7 constant_dynamic-update-slice_fusion.9
  166.4 0.7 constant_dynamic-update-slice_fusion.8
  167.1 1.6 constant_dynamic-update-slice_fusion.7
  168.7 1.6 constant_dynamic-update-slice_fusion.6
  170.3 0.7 constant_dynamic-update-slice_fusion.5
  171.0 0.7 constant_dynamic-update-slice_fusion.4
  171.7 0.7 constant_dynamic-update-slice_fusion.3
  172.4 0.7 constant_dynamic-update-slice_fusion.2
  173.1 0.7 constant_dynamic-update-slice_fusion.1
  173.8 0.7 constant_dynamic-update-slice_fusion
  174.4 43.9 %all-gather.4.cloned.1.call-done = f32[128,128,128]{2,1,0:T(8,128)} async-done(((f32[16,128,128]{2,1,0:T(8,128)}), f32[128,128,128]{2,1,0:T(8,128)}) %all-gather.4.cloned.1.call-update) | async-done | bytes 8388624 | tf_op jit(solution)/shard_map/all_gather | solution.py:13
  218.4 11.3 %while.29 = (s32[]{:T(128)}, f32[16,128,128]{2,1,0:T(8,128)S(1)}, s32[]{:T(128)}, f32[8,16,128,128]{3,2,1,0:T(8,128)}, s32[]{:T(128)}, /*index=5*/s32[]{:T(128)}) while((s32[]{:T(128)}, f32[16,128,128]{2,1,0:T(8,128)S(1)}, s32[]{:T(128)}, f32[8,16,128,128]{3,2,1,0:T(8,128)}, s32[]{:T(128)}, /*index=5*/s32[]{:T(128)}) %tuple.70), condition=%wide.region_4.5_spmd.clone, body=%wide.region_3.4_spmd.clone.sunk | while | flops 786436 | bytes 3145829 | solution.py:20
  218.4 1.6 add_select_fusion.5
  220.0 1.6 add_select_fusion.5
  221.6 1.6 add_select_fusion.5
  223.2 1.6 add_select_fusion.5
  224.8 1.6 add_select_fusion.5
  226.4 1.6 add_select_fusion.5
  228.0 1.6 add_select_fusion.5
  229.6 0.0 copy-start.8
  229.7 1.8 multiply_reduce_fusion
  231.4 0.3 multiply_convert_fusion
  231.8 1.0 copy.16
  (29 shorter events, 0.2 us)
Async XLA Ops:
  6.5 139.7 %copy-start = (bf16[128,2048]{1,0:T(8,128)(2,1)S(1)}, bf16[128,2048]{1,0:T(8,128)(2,1)}, u32[]{:S(2)}) copy-start(bf16[128,2048]{1,0:T(8,128)(2,1)} %param.8) | copy-start | bytes 1572868
  6.5 71.7 %reduce-scatter.2.cloned.1.call-start = ((), (), s32[]{:S(2)}) async-start(), calls=%async_computation.1 | async-start | bytes 1179648 | tf_op jit(solution)/shard_map/reduce_scatter | solution.py:39
  10.2 136.0 %copy-start.1 = (bf16[128,2048]{1,0:T(8,128)(2,1)S(1)}, bf16[128,2048]{1,0:T(8,128)(2,1)}, u32[]{:S(2)}) copy-start(bf16[128,2048]{1,0:T(8,128)(2,1)} %param.10) | copy-start | bytes 1572868
  10.3 208.1 %all-gather.4.cloned.1.call-start = ((), (), s32[]{:S(2)}) async-start(), calls=%async_computation.2 | async-start | bytes 9437184 | tf_op jit(solution)/shard_map/all_gather | solution.py:13
  85.7 9.7 %collective-permute-start = (f32[16,16,128]{2,1,0:T(8,128)S(1)}, f32[16,16,128]{2,1,0:T(8,128)S(1)}, u32[]{:S(2)}, u32[]{:S(2)}) collective-permute-start(f32[16,16,128]{2,1,0:T(8,128)S(1)} %get-tuple-element.163), channel_id=1, source_target_pairs={{0,1},{1,2},{2,3},{3,4},{4,5},{5,6},{6,7},{7,0},{8,9},{9,10},{10,1... | collective-permute-start | bytes 393224 | tf_op jit(solution)/shard_map/ppermute | solution.py:43
  95.4 11.0 %collective-permute-start.1 = (f32[16,16,128]{2,1,0:T(8,128)S(1)}, f32[16,16,128]{2,1,0:T(8,128)S(1)}, u32[]{:S(2)}, u32[]{:S(2)}) collective-permute-start(f32[16,16,128]{2,1,0:T(8,128)S(1)} %collective-permute-done), channel_id=1, source_target_pairs={{0,1},{1,2},{2,3},{3,4},{4,5},{5,6},{6,7},{7,0},{8,9},{9,10},{10,1... | collective-permute-start | bytes 393224 | tf_op jit(solution)/shard_map/ppermute | solution.py:43
  106.4 10.8 %collective-permute-start.2 = (f32[16,16,128]{2,1,0:T(8,128)S(1)}, f32[16,16,128]{2,1,0:T(8,128)S(1)}, u32[]{:S(2)}, u32[]{:S(2)}) collective-permute-start(f32[16,16,128]{2,1,0:T(8,128)S(1)} %collective-permute-done.1), channel_id=1, source_target_pairs={{0,1},{1,2},{2,3},{3,4},{4,5},{5,6},{6,7},{7,0},{8,9},{9,10},{10,1... | collective-permute-start | bytes 393224 | tf_op jit(solution)/shard_map/ppermute | solution.py:43
  117.2 29.7 %copy-start.2 = (f32[16,16,128]{2,1,0:T(8,128)}, f32[16,16,128]{2,1,0:T(8,128)S(1)}, u32[]{:S(2)}) copy-start(f32[16,16,128]{2,1,0:T(8,128)S(1)} %collective-permute-done.2) | copy-start | bytes 393220
  117.2 10.6 %collective-permute-start.3 = (f32[16,16,128]{2,1,0:T(8,128)S(1)}, f32[16,16,128]{2,1,0:T(8,128)S(1)}, u32[]{:S(2)}, u32[]{:S(2)}) collective-permute-start(f32[16,16,128]{2,1,0:T(8,128)S(1)} %collective-permute-done.2), channel_id=1, source_target_pairs={{0,1},{1,2},{2,3},{3,4},{4,5},{5,6},{6,7},{7,0},{8,9},{9,10},{10,1... | collective-permute-start | bytes 393224 | tf_op jit(solution)/shard_map/ppermute | solution.py:43
  127.8 19.1 %copy-start.4 = (f32[16,16,128]{2,1,0:T(8,128)}, f32[16,16,128]{2,1,0:T(8,128)S(1)}, u32[]{:S(2)}) copy-start(f32[16,16,128]{2,1,0:T(8,128)S(1)} %collective-permute-done.3) | copy-start | bytes 393220
  127.8 10.6 %collective-permute-start.4 = (f32[16,16,128]{2,1,0:T(8,128)S(1)}, f32[16,16,128]{2,1,0:T(8,128)S(1)}, u32[]{:S(2)}, u32[]{:S(2)}) collective-permute-start(f32[16,16,128]{2,1,0:T(8,128)S(1)} %collective-permute-done.3), channel_id=1, source_target_pairs={{0,1},{1,2},{2,3},{3,4},{4,5},{5,6},{6,7},{7,0},{8,9},{9,10},{10,1... | collective-permute-start | bytes 393224 | tf_op jit(solution)/shard_map/ppermute | solution.py:43
  138.4 8.5 %copy-start.6 = (f32[16,16,128]{2,1,0:T(8,128)}, f32[16,16,128]{2,1,0:T(8,128)S(1)}, u32[]{:S(2)}) copy-start(f32[16,16,128]{2,1,0:T(8,128)S(1)} %collective-permute-done.4) | copy-start | bytes 393220
  138.4 7.8 %collective-permute-start.5 = (f32[16,16,128]{2,1,0:T(8,128)S(1)}, f32[16,16,128]{2,1,0:T(8,128)}, u32[]{:S(2)}, u32[]{:S(2)}) collective-permute-start(f32[16,16,128]{2,1,0:T(8,128)S(1)} %collective-permute-done.4), channel_id=1, source_target_pairs={{0,1},{1,2},{2,3},{3,4},{4,5},{5,6},{6,7},{7,0},{8,9},{9,10},{10,1... | collective-permute-start | bytes 393224 | tf_op jit(solution)/shard_map/ppermute | solution.py:43
  146.2 10.9 %collective-permute-start.6 = (f32[16,16,128]{2,1,0:T(8,128)}, f32[16,16,128]{2,1,0:T(8,128)}, u32[]{:S(2)}, u32[]{:S(2)}) collective-permute-start(f32[16,16,128]{2,1,0:T(8,128)} %collective-permute-done.5), channel_id=1, source_target_pairs={{0,1},{1,2},{2,3},{3,4},{4,5},{5,6},{6,7},{7,0},{8,9},{9,10},{10,1... | collective-permute-start | bytes 393224 | tf_op jit(solution)/shard_map/ppermute | solution.py:43
  146.9 23.4 %copy-start.7 = (f32[16,16,128]{2,1,0:T(8,128)S(1)}, f32[16,16,128]{2,1,0:T(8,128)}, u32[]{:S(2)}) copy-start(f32[16,16,128]{2,1,0:T(8,128)} %copy-done.6) | copy-start | bytes 393220
  146.9 24.1 %copy-start.5 = (f32[16,16,128]{2,1,0:T(8,128)S(1)}, f32[16,16,128]{2,1,0:T(8,128)}, u32[]{:S(2)}) copy-start(f32[16,16,128]{2,1,0:T(8,128)} %copy-done.4) | copy-start | bytes 393220
  147.0 24.7 %copy-start.3 = (f32[16,16,128]{2,1,0:T(8,128)S(1)}, f32[16,16,128]{2,1,0:T(8,128)}, u32[]{:S(2)}) copy-start(f32[16,16,128]{2,1,0:T(8,128)} %copy-done.2) | copy-start | bytes 393220
  229.6 1.8 copy-start.8
Sparse Core Ops, SparseCore 0:
  10.7 67.4 reduce-scatter.1
  80.3 137.9 all-gather.3
